TPU v7x, 256 devices: a whole 4x4x8 slice. The times are simulated.
256 devices in a mesh: prow: 32 (over x, z), pcol: 8 (over y, core).
Axes of the slice: x: 4, y: 4, z: 8, core: 2. Of those that a mesh axis runs over, the one named last changes fastest.
Arguments:
- anc_inverse: bfloat16 [4, 32, 256, 16, 8, 256], P(None, 'prow', None, None, 'pcol'), may hold values from -6 to 6
- first_lower: bfloat16 [4, 32, 256, 256], P(None, 'prow', 'pcol'), may hold values from -0.046875 to 0.046875
- second_lower: bfloat16 [4, 32, 256, 256], P(None, 'prow', 'pcol'), may hold values from -0.0546875 to 0.0546875
- second_top: bfloat16 [256, 256], replicated, may hold values from -0.3125 to 0.3125
- struct_first: int32 [128], replicated, may hold values from 0 to 1
- struct_keep: int32 [128], replicated, may hold values from 0 to 1
- pivot_h: float32 [2, 256, 256], replicated, as said below
- pivot_s: float32 [2, 256, 256], replicated, as said below
- shifts: float32 [40], replicated, may hold values from 0.5 to 4
- pole_index: int32 [40], replicated, may hold values from 0 to 39, each once
Outputs:
- first_column: bfloat16 [4, 32, 256, 256], P(None, 'prow', 'pcol')
- first_diag: float32 [256, 256], replicated
- link_column: bfloat16 [256, 256], replicated
- second_column: bfloat16 [4, 32, 256, 256], P(None, 'prow', 'pcol')
- second_diag: float32 [256, 256], replicated
Inputs may be any that keep to these rules, and one draw needn't show every extreme that they name: `struct_first`: 1 marks a block row of the first supernode's structure. `struct_keep`: 1 marks a structure block that the second supernode keeps. `pole_index`: each pole appears once. `pivot_h`: symmetric, with a positive diagonal larger than each row's off-diagonal magnitudes together. `pivot_s`: symmetric, with a positive diagonal larger than each row's off-diagonal magnitudes together.
All inputs are finite; a program needn't handle non-finite values.
Results may differ from a plain program's by a relative error of at most 0.0041.
The roundings to bfloat16 on the way count: a program that leaves them out, or rounds other values in their place, can miss the bound.
Values may be sent and summed in bfloat16 or wider, within the bound.
A program may use at most 64 MiB of HBM per device.

v0:
```python
import jax
import jax.numpy as jnp
from jax import lax
from jax.sharding import PartitionSpec as P


def pivot_inverse(h_block, s_block, shift):
    factor = jnp.linalg.cholesky(h_block + shift * s_block)
    identity = jnp.eye(h_block.shape[0], dtype=jnp.float32)
    return jax.scipy.linalg.cho_solve((factor, True), identity)


def local_mask(flags, row_blocks, grid_rows, my_row):
    table = flags.reshape(row_blocks, grid_rows).astype(jnp.float32)
    return lax.dynamic_index_in_dim(table, my_row, axis=1, keepdims=False)


def per_device(
    anc_inverse,
    first_lower,
    second_lower,
    second_top,
    struct_first,
    struct_keep,
    pivot_h,
    pivot_s,
    shifts,
    pole_index,
):
    grid_rows = lax.axis_size("prow")
    grid_cols = lax.axis_size("pcol")
    my_row = lax.axis_index("prow")
    my_col = lax.axis_index("pcol")
    row_blocks = first_lower.shape[0]
    slab = first_lower.shape[2]
    width = first_lower.shape[3]
    col_blocks = anc_inverse.shape[3]
    first_mask = local_mask(struct_first, row_blocks, grid_rows, my_row)
    second_mask = first_mask * local_mask(struct_keep, row_blocks, grid_rows, my_row)
    lower_first = first_lower[:, 0] * first_mask.astype(jnp.bfloat16)[:, None, None]
    lower_second = second_lower[:, 0] * second_mask.astype(jnp.bfloat16)[:, None, None]
    stacked = jnp.concatenate([lower_first, lower_second], axis=2)[:, None]
    gathered = lax.all_gather(stacked, "prow", axis=1, tiled=True)
    grouped = gathered.reshape(row_blocks, grid_rows // grid_cols, grid_cols, slab, 2 * width)
    columns = lax.all_to_all(grouped, "pcol", split_axis=2, concat_axis=3, tiled=True)
    column_blocks = columns.reshape(col_blocks, width, 2 * width)
    inverse_rows = anc_inverse.reshape(row_blocks, width, col_blocks, width)
    totals = lax.psum(
        jnp.einsum(
            "axcy,cyz->xaz", inverse_rows, column_blocks, preferred_element_type=jnp.float32
        ),
        "pcol",
    )
    row_part = lax.dynamic_slice_in_dim(totals, my_col * slab, slab, 0)
    first_col = (-row_part[:, :, :width] * first_mask[None, :, None]).astype(jnp.bfloat16)
    bridge = jnp.einsum("raw,wz->raz", first_col, second_top, preferred_element_type=jnp.float32)
    second_col = (-(row_part[:, :, width:] + bridge) * second_mask[None, :, None]).astype(
        jnp.bfloat16
    )
    first_rows = lower_first.transpose(1, 0, 2)
    second_rows = lower_second.transpose(1, 0, 2)
    first_term = jnp.einsum(
        "ray,raz->yz", first_rows, first_col, preferred_element_type=jnp.float32
    )
    cross_term = jnp.einsum(
        "ray,raz->yz", first_col, second_rows, preferred_element_type=jnp.float32
    )
    second_term = jnp.einsum(
        "ray,raz->yz", second_rows, second_col, preferred_element_type=jnp.float32
    )
    first_sum, cross_sum, second_sum = lax.psum(
        (first_term, cross_term, second_term), ("prow", "pcol")
    )
    poles = jnp.arange(shifts.shape[0], dtype=jnp.int32)
    shift = jnp.sum(jnp.where(poles == pole_index[0], shifts, 0.0))
    first_diag = pivot_inverse(pivot_h[0], pivot_s[0], shift) - first_sum
    link_col = (
        -(
            cross_sum
            + jnp.dot(
                first_diag.astype(jnp.bfloat16), second_top, preferred_element_type=jnp.float32
            )
        )
    ).astype(jnp.bfloat16)
    second_diag = (
        pivot_inverse(pivot_h[1], pivot_s[1], shift)
        - second_sum
        - jnp.einsum("yz,yw->zw", second_top, link_col, preferred_element_type=jnp.float32)
    )
    return (
        first_col.transpose(1, 0, 2)[:, None],
        first_diag,
        link_col,
        second_col.transpose(1, 0, 2)[:, None],
        second_diag,
    )


def solution(mesh):
    return jax.shard_map(
        per_device,
        mesh=mesh,
        in_specs=(
            P(None, "prow", None, None, "pcol", None),
            P(None, "prow", "pcol", None),
            P(None, "prow", "pcol", None),
            P(),
            P(),
            P(),
            P(),
            P(),
            P(),
            P(),
        ),
        out_specs=(P(None, "prow", "pcol", None), P(), P(), P(None, "prow", "pcol", None), P()),
        check_vma=False,
    )
```

profile of v0, /device:TPU:8, one launch (start us, length us, event | category | flops | bytes accessed | tf_op | source)
XLA Modules:
  0.0 544.1 jit_solution(14048645056738182097)
XLA Ops:
  7.2 0.7 convert_element_type.47
  8.0 0.7 convert_element_type.44
  9.0 0.9 bitcast_multiply_fusion
  9.9 0.9 bitcast_multiply_fusion.1
  10.8 0.7 pad_maximum_fusion
  11.5 1.1 fusion.48
  12.7 1.1 fusion.47
  13.9 1.9 fusion.43
  15.8 0.7 fusion.23
  16.9 0.7 fusion.22
  17.7 0.7 fusion.11
  18.5 11.7 %cholesky.130 = f32[128,128]{1,0:T(8,128)S(1)} custom-call(f32[128,128]{1,0:T(8,128)S(1)} %cholesky.194), custom_call_target="Cholesky" | custom-call | tf_op jit(solution)/shard_map/jit(cholesky)/cholesky | solution.py:8
  30.3 9.8 %custom-call.15 = f32[1,128,128]{1,2,0:T(8,128)S(1)} custom-call(f32[1,128,128]{2,1,0:T(8,128)S(1)} %get-tuple-element.84), custom_call_target="InvertDiagBlocksLowerTriangular" | custom-call | tf_op jit(solution)/shard_map/jit(cholesky)/cholesky | solution.py:8
  40.6 11.7 %cholesky.147 = f32[128,128]{1,0:T(8,128)S(1)} custom-call(f32[128,128]{1,0:T(8,128)S(1)} %convolution_subtract_fusion.5), custom_call_target="Cholesky" | custom-call | tf_op jit(solution)/shard_map/jit(cholesky)/cholesky | solution.py:8
  52.3 0.6 compare_reduce_fusion.3
  53.0 0.6 compare_reduce_fusion.2
  55.0 41.5 %all-gather.3.cloned.1.call-done = bf16[4,1024,512]{2,1,0:T(8,128)(2,1)} async-done(((bf16[4,32,512]{2,1,0:T(8,128)(2,1)}), bf16[4,1024,512]{2,1,0:T(8,128)(2,1)}) %all-gather.3.cloned.1.call-update) | async-done | bytes 4194320 | tf_op jit(solution)/shard_map/all_gather | solution.py:43
  96.5 4.7 copy.82
  101.2 5.2 all-to-all-start
  106.4 4.0 while.4
  106.5 0.6 fusion.74
  107.0 1.4 bitcast_dynamic-update-slice_fusion.4
  108.5 0.6 fusion.74
  109.0 1.4 bitcast_dynamic-update-slice_fusion.4
  110.4 19.7 %custom-call.16 = f32[2,128,128]{1,2,0:T(8,128)S(1)} custom-call(f32[2,128,128]{2,1,0:T(8,128)S(1)} %get-tuple-element.21), custom_call_target="InvertDiagBlocksLowerTriangular" | custom-call | tf_op jit(solution)/shard_map/jit(_cho_solve)/triangular_solve | solution.py:10
  130.1 11.7 %cholesky.164 = f32[128,128]{1,0:T(8,128)S(1)} custom-call(f32[128,128]{1,0:T(8,128)S(1)} %cholesky.197), custom_call_target="Cholesky" | custom-call | tf_op jit(solution)/shard_map/jit(cholesky)/cholesky | solution.py:8
  141.9 9.8 %custom-call.17 = f32[1,128,128]{1,2,0:T(8,128)S(1)} custom-call(f32[1,128,128]{2,1,0:T(8,128)S(1)} %get-tuple-element.80), custom_call_target="InvertDiagBlocksLowerTriangular" | custom-call | tf_op jit(solution)/shard_map/jit(cholesky)/cholesky | solution.py:8
  152.2 11.7 %cholesky.181 = f32[128,128]{1,0:T(8,128)S(1)} custom-call(f32[128,128]{1,0:T(8,128)S(1)} %convolution_subtract_fusion.4), custom_call_target="Cholesky" | custom-call | tf_op jit(solution)/shard_map/jit(cholesky)/cholesky | solution.py:8
  163.9 0.6 compare_reduce_fusion.1
  164.6 0.6 compare_reduce_fusion
  166.6 4.0 while.5
  167.2 1.4 bitcast_dynamic-update-slice_fusion.5
  168.6 0.6 fusion.75
  169.2 1.4 bitcast_dynamic-update-slice_fusion.5
  170.6 19.9 %custom-call.18 = f32[2,128,128]{1,2,0:T(8,128)S(1)} custom-call(f32[2,128,128]{2,1,0:T(8,128)S(1)} %get-tuple-element.22), custom_call_target="InvertDiagBlocksLowerTriangular" | custom-call | tf_op jit(solution)/shard_map/jit(_cho_solve)/triangular_solve | solution.py:10
  192.3 2.5 copy.83
  194.8 9.6 %fusion.2 = f32[256,4,512]{2,0,1:T(8,128)} fusion(bf16[16,256,512,1]{2,1,0,3:T(8,128)(2,1)S(1)} %bitcast.134, bf16[4,256,16,256]{3,2,1,0:T(8,128)(2,1)} %bitcast.136), kind=kOutput, calls=%fused_computation.6 | convolution fusion | flops 4294967296 | bytes 14680064 | tf_op jit(solution)/shard_map/axcy,cyz->xaz/dot_general | solution.py:49
  206.0 64.4 %all-reduce.5.cloned.1.call-done = f32[256,4,512]{2,0,1:T(8,128)} async-done(((f32[256,4,512]{2,0,1:T(8,128)}), f32[256,4,512]{2,0,1:T(8,128)}) %all-reduce.5.cloned.1.call-update) | async-done | bytes 2097168 | tf_op jit(solution)/shard_map/psum | solution.py:48
  270.3 1.0 fusion.15
  271.3 0.9 convolution_bitcast_fusion.3
  272.2 0.9 convolution_bitcast_fusion.2
  273.1 1.1 fusion.10
  274.2 0.9 convolution_bitcast_fusion.1
  275.5 1.6 fusion.71
  277.1 256.3 %all-reduce.7.cloned.1.call-done = (f32[256,256]{1,0:T(8,128)}, f32[256,256]{1,0:T(8,128)}, f32[256,256]{1,0:T(8,128)}) async-done(((f32[256,256]{1,0:T(8,128)}, f32[256,256]{1,0:T(8,128)}, f32[256,256]{1,0:T(8,128)}), (f32[256,256]{1,0:T(8,128)}, f32[256,256]{1,0:T(8,128)}, f32[256,256]{1,0:T(8,128)})) %all-reduce.7.cloned.1.call-update) | async-done | bytes 786448 | tf_op jit(solution)/shard_map/psum | solution.py:71
  533.4 1.0 maximum_subtract_fusion
  534.4 1.2 fusion.7
  535.6 1.9 fusion.6
  (61 shorter events, 6.7 us)
Async XLA Ops:
  7.2 266.0 %copy-start = (bf16[256,256]{1,0:T(8,128)(2,1)S(1)}, bf16[256,256]{1,0:T(8,128)(2,1)}, u32[]{:S(2)}) copy-start(bf16[256,256]{1,0:T(8,128)(2,1)} %param.16) | copy-start | bytes 393220
  7.2 89.3 %all-gather.3.cloned.1.call-start = ((), (), s32[]{:S(2)}) async-start(), calls=%async_computation.2 | async-start | bytes 4325376 | tf_op jit(solution)/shard_map/all_gather | solution.py:43
  101.2 91.1 %all-to-all-start = ((bf16[4,4,8,32,512]{4,3,1,0,2:T(8,128)(2,1)}), bf16[4,4,8,32,512]{4,3,1,0,2:T(8,128)(2,1)}, u32[]{:S(2)}, u32[]{:S(2)}) async-start(bf16[4,4,8,32,512]{4,3,1,0,2:T(8,128)(2,1)} %copy.82), calls=%async_computation | async-start | bytes 8388608 | tf_op jit(solution)/shard_map/all_to_all | solution.py:45
  106.4 164.0 %all-reduce.5.cloned.1.call-start = ((), (), s32[]{:S(2)}) async-start(), calls=%async_computation.1 | async-start | bytes 4194304 | tf_op jit(solution)/shard_map/psum | solution.py:48
  204.4 329.0 %all-reduce.7.cloned.1.call-start = ((), (), s32[]{:S(2)}) async-start(), calls=%async_computation.3 | async-start | bytes 1572864 | tf_op jit(solution)/shard_map/psum | solution.py:71
  274.2 263.3 %copy-start.3 = (bf16[32,4,256]{2,0,1:T(8,128)(2,1)}, bf16[32,4,256]{2,0,1:T(8,128)(2,1)S(1)}, u32[]{:S(2)}) copy-start(bf16[32,4,256]{2,0,1:T(8,128)(2,1)S(1)} %fusion.10) | copy-start | bytes 196612
  534.4 3.2 copy-start.1
  535.6 2.0 copy-start.2
Sparse Core Ops, SparseCore 0:
  11.6 84.8 all-gather.2
  204.5 65.7 all-reduce.4
  276.7 256.6 all-reduce.6
where the time goes:
time: 545 us; the launch traced here: 544 us
  waiting for transfers between devices  362 us (66%)
  other arithmetic  120 us (22%)
  matrix products  20.9 us (4%)
  local copies, waits for them, and re-layouts  18.6 us (3%)
  between operations  16.7 us (3%)
    psum x1, waiting for transfers between devices, per_device(): lax.psum((first_term, cross_term, second_term), ('prow', 'pcol'))  256 us
    another operation x14, other arithmetic, pivot_inverse(): factor = jnp.linalg.cholesky(h_block + shift * s_block)  69.2 us
    psum x1, waiting for transfers between devices, per_device(): lax.psum(jnp.einsum('axcy,cyz->xaz', inverse_rows, column_blocks, preferr...  64.4 us
    all_gather x1, waiting for transfers between devices, per_device(): gathered = lax.all_gather(stacked, 'prow', axis=1, tiled=True)  41.5 us
    another operation x5, other arithmetic, pivot_inverse(): return jax.scipy.linalg.cho_solve((factor, True), identity)  39.6 us
  transfers between devices with their start and end apart: 4, of which 3 were waited for; matrix products, arithmetic and copies ran while one was open for 24% of the time, Pallas kernels for 0%

commit v1 on v0

--- a/solution.py
+++ b/solution.py
@@ -69,7 +69,7 @@
         "ray,raz->yz", second_rows, second_col, preferred_element_type=jnp.float32
     )
     first_sum, cross_sum, second_sum = lax.psum(
-        (first_term, cross_term, second_term), ("prow", "pcol")
+        lax.psum((first_term, cross_term, second_term), axis_name="prow"), axis_name="pcol"
     )
     poles = jnp.arange(shifts.shape[0], dtype=jnp.int32)
     shift = jnp.sum(jnp.where(poles == pole_index[0], shifts, 0.0))

time: 545 us -> 485 us (0.89)
  waiting for transfers between devices: 362 us -> 301 us
    psum x1 -> x2, waiting for transfers between devices: 256 us -> 212 us  [the longest x1 150 us: per_device(): lax.psum((first_term, cross_term, second_term), axis_name='prow')]
    psum x1, waiting for transfers between devices: 64.4 us -> 44.7 us  [per_device(): lax.psum(jnp.einsum('axcy,cyz->xaz', inverse_rows, column_blocks, preferr...]
  transfers between devices with their start and end apart: 4 -> 5, of which waited for: 3 -> 4; matrix products, arithmetic and copies ran while one was open for 24% -> 27% of each run, Pallas kernels for 0% -> 0%
where the time goes in v1:
time: 485 us; the launch traced here: 482 us
  waiting for transfers between devices  301 us (62%)
  other arithmetic  120 us (25%)
  matrix products  21.2 us (4%)
  local copies, waits for them, and re-layouts  18.6 us (4%)
  between operations  16.8 us (3%)
  starting transfers between devices  5.09 us (1%)
    psum x1, waiting for transfers between devices, per_device(): lax.psum((first_term, cross_term, second_term), axis_name='prow')  150 us
    another operation x14, other arithmetic, pivot_inverse(): factor = jnp.linalg.cholesky(h_block + shift * s_block)  69.2 us
    psum x1, waiting for transfers between devices, per_device(): lax.psum(lax.psum((first_term, cross_term, second_term), axis_name='prow'...  62.4 us
    psum x1, waiting for transfers between devices, per_device(): lax.psum(jnp.einsum('axcy,cyz->xaz', inverse_rows, column_blocks, preferr...  44.7 us
    all_gather x1, waiting for transfers between devices, per_device(): gathered = lax.all_gather(stacked, 'prow', axis=1, tiled=True)  43.5 us
    another operation x5, other arithmetic, pivot_inverse(): return jax.scipy.linalg.cho_solve((factor, True), identity)  39.4 us
    dot_general x1, matrix products, per_device(): jnp.einsum('axcy,cyz->xaz', inverse_rows, column_blocks, preferred_elemen...  9.8 us
  transfers between devices with their start and end apart: 5, of which 4 were waited for; matrix products, arithmetic and copies ran while one was open for 27% of the time, Pallas kernels for 0%

profile of v1, /device:TPU:8, one launch (start us, length us, event | category | flops | bytes accessed | tf_op | source)
XLA Modules:
  0.0 482.4 jit_solution(2449880050066863502)
XLA Ops:
  7.2 0.7 convert_element_type.47
  8.0 0.7 convert_element_type.44
  9.0 0.9 bitcast_multiply_fusion
  9.9 0.9 bitcast_multiply_fusion.1
  10.8 0.7 pad_maximum_fusion
  11.5 1.1 fusion.48
  12.7 1.1 fusion.47
  13.9 1.9 fusion.43
  15.8 0.7 fusion.23
  16.9 0.7 fusion.22
  17.7 0.7 fusion.11
  18.5 11.7 %cholesky.130 = f32[128,128]{1,0:T(8,128)S(1)} custom-call(f32[128,128]{1,0:T(8,128)S(1)} %cholesky.194), custom_call_target="Cholesky" | custom-call | tf_op jit(solution)/shard_map/jit(cholesky)/cholesky | solution.py:8
  30.3 9.8 %custom-call.15 = f32[1,128,128]{1,2,0:T(8,128)S(1)} custom-call(f32[1,128,128]{2,1,0:T(8,128)S(1)} %get-tuple-element.87), custom_call_target="InvertDiagBlocksLowerTriangular" | custom-call | tf_op jit(solution)/shard_map/jit(cholesky)/cholesky | solution.py:8
  40.6 11.7 %cholesky.147 = f32[128,128]{1,0:T(8,128)S(1)} custom-call(f32[128,128]{1,0:T(8,128)S(1)} %convolution_subtract_fusion.5), custom_call_target="Cholesky" | custom-call | tf_op jit(solution)/shard_map/jit(cholesky)/cholesky | solution.py:8
  52.3 0.6 compare_reduce_fusion.3
  53.0 43.5 %all-gather.3.cloned.1.call-done = bf16[4,1024,512]{2,1,0:T(8,128)(2,1)} async-done(((bf16[4,32,512]{2,1,0:T(8,128)(2,1)}), bf16[4,1024,512]{2,1,0:T(8,128)(2,1)}) %all-gather.3.cloned.1.call-update) | async-done | bytes 4194320 | tf_op jit(solution)/shard_map/all_gather | solution.py:43
  96.5 4.7 copy.82
  101.2 5.0 %all-to-all-start = ((bf16[4,4,8,32,512]{4,3,1,0,2:T(8,128)(2,1)}), bf16[4,4,8,32,512]{4,3,1,0,2:T(8,128)(2,1)}, u32[]{:S(2)}, u32[]{:S(2)}) async-start(bf16[4,4,8,32,512]{4,3,1,0,2:T(8,128)(2,1)} %copy.82), calls=%async_computation | async-start | bytes 8388608 | tf_op jit(solution)/shard_map/all_to_all | solution.py:45
  106.2 0.6 compare_reduce_fusion.2
  108.2 4.0 while.4
  108.3 0.6 fusion.74
  108.8 1.4 bitcast_dynamic-update-slice_fusion.4
  110.3 0.6 fusion.74
  110.9 1.4 bitcast_dynamic-update-slice_fusion.4
  112.2 19.7 %custom-call.16 = f32[2,128,128]{1,2,0:T(8,128)S(1)} custom-call(f32[2,128,128]{2,1,0:T(8,128)S(1)} %get-tuple-element.21), custom_call_target="InvertDiagBlocksLowerTriangular" | custom-call | tf_op jit(solution)/shard_map/jit(_cho_solve)/triangular_solve | solution.py:10
  131.9 11.7 %cholesky.164 = f32[128,128]{1,0:T(8,128)S(1)} custom-call(f32[128,128]{1,0:T(8,128)S(1)} %cholesky.197), custom_call_target="Cholesky" | custom-call | tf_op jit(solution)/shard_map/jit(cholesky)/cholesky | solution.py:8
  143.7 9.8 %custom-call.17 = f32[1,128,128]{1,2,0:T(8,128)S(1)} custom-call(f32[1,128,128]{2,1,0:T(8,128)S(1)} %get-tuple-element.83), custom_call_target="InvertDiagBlocksLowerTriangular" | custom-call | tf_op jit(solution)/shard_map/jit(cholesky)/cholesky | solution.py:8
  154.0 11.7 %cholesky.181 = f32[128,128]{1,0:T(8,128)S(1)} custom-call(f32[128,128]{1,0:T(8,128)S(1)} %convolution_subtract_fusion.4), custom_call_target="Cholesky" | custom-call | tf_op jit(solution)/shard_map/jit(cholesky)/cholesky | solution.py:8
  165.7 0.6 compare_reduce_fusion.1
  166.4 0.6 compare_reduce_fusion
  169.0 4.0 while.5
  169.6 1.4 bitcast_dynamic-update-slice_fusion.5
  171.6 1.4 bitcast_dynamic-update-slice_fusion.5
  173.0 2.5 copy.83
  175.5 9.8 %fusion.2 = f32[256,4,512]{2,0,1:T(8,128)} fusion(bf16[16,256,512,1]{2,1,0,3:T(8,128)(2,1)S(1)} %bitcast.134, bf16[4,256,16,256]{3,2,1,0:T(8,128)(2,1)} %bitcast.136), kind=kOutput, calls=%fused_computation.6 | convolution fusion | flops 4294967296 | bytes 14680064 | tf_op jit(solution)/shard_map/axcy,cyz->xaz/dot_general | solution.py:49
  185.7 19.7 %custom-call.18 = f32[2,128,128]{1,2,0:T(8,128)S(1)} custom-call(f32[2,128,128]{2,1,0:T(8,128)S(1)} %get-tuple-element.22), custom_call_target="InvertDiagBlocksLowerTriangular" | custom-call | tf_op jit(solution)/shard_map/jit(_cho_solve)/triangular_solve | solution.py:10
  206.6 44.7 %all-reduce.7.cloned.1.call-done = f32[256,4,512]{2,0,1:T(8,128)} async-done(((f32[256,4,512]{2,0,1:T(8,128)}), f32[256,4,512]{2,0,1:T(8,128)}) %all-reduce.7.cloned.1.call-update) | async-done | bytes 2097168 | tf_op jit(solution)/shard_map/psum | solution.py:48
  251.3 1.0 fusion.15
  252.3 0.9 convolution_bitcast_fusion.3
  253.2 0.9 convolution_bitcast_fusion.2
  254.1 1.1 fusion.10
  255.2 0.9 convolution_bitcast_fusion.1
  257.4 149.9 %all-reduce.9.cloned.1.call-done = (f32[256,256]{1,0:T(8,128)}, f32[256,256]{1,0:T(8,128)}, f32[256,256]{1,0:T(8,128)}) async-done(((f32[256,256]{1,0:T(8,128)}, f32[256,256]{1,0:T(8,128)}, f32[256,256]{1,0:T(8,128)}), (f32[256,256]{1,0:T(8,128)}, f32[256,256]{1,0:T(8,128)}, f32[256,256]{1,0:T(8,128)})) %all-reduce.9.cloned.1.call-update) | async-done | bytes 786448 | tf_op jit(solution)/shard_map/psum | solution.py:72
  407.6 1.6 fusion.71
  409.2 62.4 %all-reduce.11.cloned.1.call-done = (f32[256,256]{1,0:T(8,128)}, f32[256,256]{1,0:T(8,128)}, f32[256,256]{1,0:T(8,128)}) async-done(((f32[256,256]{1,0:T(8,128)}, f32[256,256]{1,0:T(8,128)}, f32[256,256]{1,0:T(8,128)}), (f32[256,256]{1,0:T(8,128)}, f32[256,256]{1,0:T(8,128)}, f32[256,256]{1,0:T(8,128)})) %all-reduce.11.cloned.1.call-update) | async-done | bytes 786448 | tf_op jit(solution)/shard_map/psum | solution.py:71
  471.6 1.0 maximum_subtract_fusion
  472.6 1.2 fusion.7
  473.9 1.9 fusion.6
  (64 shorter events, 7.3 us)
Async XLA Ops:
  7.2 247.0 %copy-start = (bf16[256,256]{1,0:T(8,128)(2,1)S(1)}, bf16[256,256]{1,0:T(8,128)(2,1)}, u32[]{:S(2)}) copy-start(bf16[256,256]{1,0:T(8,128)(2,1)} %param.16) | copy-start | bytes 393220
  7.2 89.3 %all-gather.3.cloned.1.call-start = ((), (), s32[]{:S(2)}) async-start(), calls=%async_computation.2 | async-start | bytes 4325376 | tf_op jit(solution)/shard_map/all_gather | solution.py:43
  101.2 71.8 %all-to-all-start = ((bf16[4,4,8,32,512]{4,3,1,0,2:T(8,128)(2,1)}), bf16[4,4,8,32,512]{4,3,1,0,2:T(8,128)(2,1)}, u32[]{:S(2)}, u32[]{:S(2)}) async-start(bf16[4,4,8,32,512]{4,3,1,0,2:T(8,128)(2,1)} %copy.82), calls=%async_computation | async-start | bytes 8388608 | tf_op jit(solution)/shard_map/all_to_all | solution.py:45
  106.2 145.1 %all-reduce.7.cloned.1.call-start = ((), (), s32[]{:S(2)}) async-start(), calls=%async_computation.1 | async-start | bytes 4194304 | tf_op jit(solution)/shard_map/psum | solution.py:48
  185.4 221.9 %all-reduce.9.cloned.1.call-start = ((), (), s32[]{:S(2)}) async-start(), calls=%async_computation.3 | async-start | bytes 1572864 | tf_op jit(solution)/shard_map/psum | solution.py:72
  255.2 220.6 %copy-start.3 = (bf16[32,4,256]{2,0,1:T(8,128)(2,1)}, bf16[32,4,256]{2,0,1:T(8,128)(2,1)S(1)}, u32[]{:S(2)}) copy-start(bf16[32,4,256]{2,0,1:T(8,128)(2,1)S(1)} %fusion.10) | copy-start | bytes 196612
  256.2 215.4 %all-reduce.11.cloned.1.call-start = ((), (), s32[]{:S(2)}) async-start(), calls=%async_computation.4 | async-start | bytes 1572864 | tf_op jit(solution)/shard_map/psum | solution.py:71
  472.6 3.2 copy-start.1
  473.9 2.0 copy-start.2
Sparse Core Ops, SparseCore 0:
  11.6 84.8 all-gather.2
  185.5 65.7 all-reduce.6
  256.3 150.9 all-reduce.8
  409.7 61.8 all-reduce.10
